TPU v7x, 512 devices: a whole 4x8x8 slice. The times are simulated.
512 devices in a mesh: cam: 32 (over y, x_hi, core), head: 16 (over x_lo, z).
Axes of the slice: x: 4 (x_hi: 2, x_lo: 2; x = x_hi * 2 + x_lo), y: 8, z: 8, core: 2. Of those that a mesh axis runs over, the one named last changes fastest.
Arguments:
- queries: bfloat16 [65536, 4096], P('cam', 'head'), may hold values from -24 to 24
- keys: bfloat16 [65536, 4096], P('cam', 'head'), may hold values from -24 to 24
- values: bfloat16 [65536, 4096], P('cam', 'head'), may hold values from -6 to 6
- rates: float32 [65536, 16], P('cam', 'head'), may hold values from 0.1 to 1
- w_one: bfloat16 [16, 256, 256], P('head'), may hold values from -0.375 to 0.375
- w_three: bfloat16 [16, 256, 256], P('head'), may hold values from -0.375 to 0.375
- w_two: bfloat16 [16, 256, 256], P('head'), may hold values from -0.375 to 0.375
- gain: float32 [4096], P('head'), may hold values from 0.5 to 1.5
- order: int32 [32, 2048], P('cam'), may hold values from 0 to 2047, as said below
Outputs:
- mixed: bfloat16 [65536, 4096], P('cam', 'head')
Inputs may be any that keep to these rules, and one draw needn't show every extreme that they name: `order`: each row is an ordering of 0 to 2047; every timestamp holds exactly 32 tokens of every camera.
All inputs are finite; a program needn't handle non-finite values.
Results may differ from a plain program's by a relative error of at most 0.0085.
Values may be sent and summed in bfloat16 or wider, within the bound.
A program may use at most 64 MiB of HBM per device.

v0:
```python
import jax
import jax.numpy as jnp
from jax import lax
from jax.sharding import PartitionSpec as P

PATCHES = 32


EPSILON = 1e-06


def in_one_piece(arrays, axis, split_dim, concat_dim, along):
    widths = [a.shape[along] for a in arrays]
    both = jnp.concatenate(arrays, axis=along)
    whole = lax.all_to_all(both, axis, split_axis=split_dim, concat_axis=concat_dim, tiled=True)
    return tuple(jnp.split(whole, [sum(widths[:k]) for k in range(1, len(widths))], axis=along))


def split_up(shard, dim, devices):
    dims = shard.shape
    blocks = shard.reshape(*dims[:dim], devices, dims[dim] // devices, *dims[dim + 1 :])
    return jnp.moveaxis(blocks, dim, 0)


def sum_at_owner(shard, axis, dim):
    devices = lax.axis_size(axis)
    blocks = lax.all_to_all(split_up(shard, dim, devices), axis, 0, 0, tiled=True)
    return jnp.sum(blocks, axis=0)


def sent_together(arrays, axis, dim, along):
    widths = [a.shape[along] for a in arrays]
    both = jnp.concatenate(arrays, axis=along)
    whole = sum_at_owner(both, axis, dim)
    return tuple(jnp.split(whole, [sum(widths[:k]) for k in range(1, len(widths))], axis=along))


def sent_to_all(shard, axis):
    devices = lax.axis_size(axis)
    return lax.all_to_all(
        jnp.broadcast_to(shard[None], (devices, *shard.shape)), axis, 0, 0, tiled=True
    )


def of_everyone(shard, axis):
    everything = sent_to_all(shard, axis)
    return jnp.sum(everything, axis=0)


def together(arrays, axis):
    vector, at, gathered = (jnp.concatenate([a.reshape(-1) for a in arrays]), 0, [])
    so_far = of_everyone(vector, axis)
    for a in arrays:
        gathered.append(so_far[at : at + a.size].reshape(a.shape))
        at += a.size
    return tuple(gathered)


def in_one_piece_2(arrays, axis, dim, along):
    both = jnp.concatenate(arrays, axis=along)
    whole, at, gathered = (lax.all_gather(both, axis, axis=dim, tiled=True), 0, [])
    for a in arrays:
        gathered.append(lax.slice_in_dim(whole, at, at + a.shape[along], axis=along))
        at += a.shape[along]
    return tuple(gathered)


def hidden_parts(tokens, first, third):
    h_one = jnp.einsum("nhd,hkd->nhk", tokens, first, preferred_element_type=jnp.float32)
    h_three = jnp.einsum("nhd,hkd->nhk", tokens, third, preferred_element_type=jnp.float32)
    return (h_one, h_three)


def gradients(key_rows, value_rows, rates, first, third, second):
    h_one, h_three = hidden_parts(key_rows, first, third)
    sigma = jax.nn.sigmoid(h_one)
    active = (h_one * sigma * h_three).astype(jnp.bfloat16)
    error = (-rates[:, :, None] * value_rows.astype(jnp.float32)).astype(jnp.bfloat16)
    grad_second = jnp.einsum("nhd,nhk->hdk", error, active, preferred_element_type=jnp.float32)
    back = jnp.einsum("nhd,hdk->nhk", error, second, preferred_element_type=jnp.float32)
    back_one = (back * h_three * sigma * (1.0 + h_one * (1.0 - sigma))).astype(jnp.bfloat16)
    back_three = (back * h_one * sigma).astype(jnp.bfloat16)
    grad_first = jnp.einsum("nhk,nhd->hkd", back_one, key_rows, preferred_element_type=jnp.float32)
    grad_third = jnp.einsum(
        "nhk,nhd->hkd", back_three, key_rows, preferred_element_type=jnp.float32
    )
    return (grad_first, grad_third, grad_second)


def weight_scale(weight):
    wf = weight.astype(jnp.float32)
    return jnp.sqrt(jnp.mean(wf * wf, axis=(1, 2)))


def renew(weight, grad, weight_rms, grad_total, entries):
    wf = weight.astype(jnp.float32)
    scale = weight_rms / jnp.sqrt(grad_total / entries + EPSILON)
    moved = wf - scale[:, None, None] * grad
    ratio = jnp.sqrt(jnp.sum(wf * wf, axis=-1, keepdims=True)) / jnp.sqrt(
        jnp.sum(moved * moved, axis=-1, keepdims=True) + EPSILON
    )
    return (moved * ratio).astype(jnp.bfloat16)


def attend(parts, local, head_size):
    query_all, key_all, value_all = parts
    cams, frames, patches, width = query_all.shape

    def one_frame(blocks):
        query_block, key_block, value_block = blocks
        query_rows = query_block.reshape(cams * patches, local, head_size)
        key_rows = key_block.reshape(cams * patches, local, head_size)
        value_rows = value_block.reshape(cams * patches, local, head_size)
        scores = jnp.einsum(
            "qhd,khd->hqk", query_rows, key_rows, preferred_element_type=jnp.float32
        ) * head_size ** (-0.5)
        scores = scores - jnp.max(scores, axis=-1, keepdims=True)
        expo = jnp.exp(scores)
        probs = (expo / jnp.sum(expo, axis=-1, keepdims=True)).astype(jnp.bfloat16)
        result = jnp.einsum("hqk,khd->qhd", probs, value_rows, preferred_element_type=jnp.float32)
        return result.astype(jnp.bfloat16).reshape(cams, patches, width)

    moved = (
        jnp.moveaxis(query_all, 1, 0),
        jnp.moveaxis(key_all, 1, 0),
        jnp.moveaxis(value_all, 1, 0),
    )
    return jnp.moveaxis(lax.map(one_frame, moved), 0, 1)


def per_device(queries, keys, values, rates, w_one, w_three, w_two, gain, order):
    count, width = queries.shape
    local = w_one.shape[0]
    head_size = w_one.shape[2]
    cams = lax.axis_size("cam")
    owned = count // (cams * PATCHES)
    slots = order[0]
    inverse = jnp.zeros((count,), jnp.int32).at[slots].set(jnp.arange(count, dtype=jnp.int32))
    sorted_query = jnp.take(queries, inverse, axis=0).reshape(cams, owned, PATCHES, width)
    sorted_keys = jnp.take(keys, inverse, axis=0).reshape(cams, owned, PATCHES, width)
    sorted_value = jnp.take(values, inverse, axis=0).reshape(cams, owned, PATCHES, width)
    arrived = in_one_piece((sorted_query, sorted_keys, sorted_value), "cam", 0, 0, 1)
    returned = lax.all_to_all(
        attend(arrived, local, head_size), "cam", split_axis=0, concat_axis=0, tiled=True
    )
    attended = jnp.take(returned.reshape(count, width), slots, axis=0)
    key_rows = keys.reshape(count, local, head_size)
    value_rows = values.reshape(count, local, head_size)
    grad_first, grad_third, grad_second = gradients(
        key_rows, value_rows, rates, w_one, w_three, w_two
    )
    weights = (w_one, w_three, w_two)
    scales = tuple((weight_scale(weight) for weight in weights))
    rows_first, rows_third, rows_second = sent_together(
        (grad_first, grad_third, grad_second), "cam", 1, 0
    )
    sq_first = jnp.sum(rows_first * rows_first, axis=(1, 2))
    sq_third = jnp.sum(rows_third * rows_third, axis=(1, 2))
    sq_second = jnp.sum(rows_second * rows_second, axis=(1, 2))
    totals = together((sq_first, sq_third, sq_second), "cam")
    renewed = []
    for weight, grad, scale_now, total in zip(
        weights, (rows_first, rows_third, rows_second), scales, totals
    ):
        rows = grad.shape[1]
        own_rows = lax.dynamic_slice_in_dim(weight, lax.axis_index("cam") * rows, rows, 1)
        renewed.append(renew(own_rows, grad, scale_now, total, weight.shape[1] * weight.shape[2]))
    renewed_first, renewed_third, renewed_second = renewed
    new_first, new_third, new_second = in_one_piece_2(
        (renewed_first, renewed_third, renewed_second), "cam", 1, 0
    )
    query_rows = queries.reshape(count, local, head_size)
    q_one, q_three = hidden_parts(query_rows, new_first, new_third)
    q_active = (q_one * jax.nn.sigmoid(q_one) * q_three).astype(jnp.bfloat16)
    readout = jnp.einsum(
        "nhk,hdk->nhd", q_active, new_second, preferred_element_type=jnp.float32
    ).reshape(count, width)
    total_sq = of_everyone(jnp.sum(readout * readout, axis=1), "head")
    full_width = width * lax.axis_size("head")
    inv_norm = 1.0 / jnp.sqrt(total_sq / full_width + EPSILON)
    mixed = readout * inv_norm[:, None] * gain[None, :] + attended.astype(jnp.float32)
    return mixed.astype(jnp.bfloat16)


def solution(mesh):
    in_specs = (
        P("cam", "head"),
        P("cam", "head"),
        P("cam", "head"),
        P("cam", "head"),
        P("head", None, None),
        P("head", None, None),
        P("head", None, None),
        P("head"),
        P("cam", None),
    )
    out_specs = P("cam", "head")
    return jax.shard_map(
        per_device, mesh=mesh, in_specs=in_specs, out_specs=out_specs, check_vma=False
    )
```

profile of v0, /device:TPU:1, one launch (start us, length us, event | category | flops | bytes accessed | tf_op | source)
XLA Modules:
  0.0 272.0 jit_solution(3477747313986220636)
XLA Ops:
  0.0 0.8 neg.17
  0.8 1.5 copy.60
  4.6 0.7 convolution_bitcast_fusion.7
  5.3 0.9 convolution_bitcast_fusion.8
  6.3 0.9 convolution_bitcast_fusion.6
  7.2 0.9 copy.62
  8.2 11.3 %all-to-all-start = ((f32[32,3,8,256]{3,2,1,0:T(8,128)}), f32[32,3,8,256]{3,2,1,0:T(8,128)}, u32[]{:S(2)}, u32[]{:S(2)}) async-start(f32[32,3,8,256]{3,2,1,0:T(8,128)} %copy.62), calls=%async_computation | async-start | bytes 1572864 | tf_op jit(solution)/shard_map/all_to_all | solution.py:27
  19.5 8.0 %scatter_custom_fusion = s32[2048]{0:T(1024)S(1)} fusion(s32[2048]{0:T(1024)S(1)} %bitcast.182, s32[2048]{0:T(1024)S(1)} %iota.3, s32[]{:T(128)} %copy.92), kind=kCustom, calls=%fused_computation.87 | custom fusion | bytes 8196 | tf_op jit(solution)/shard_map/scatter | solution.py:138
  27.6 9.0 %gather_fusion.2 = bf16[2048,256]{1,0:T(8,128)(2,1)} fusion(bf16[2048,256]{1,0:T(8,128)(2,1)S(1)} %copy-done.1, s32[2048]{0:T(1024)S(1)} %fusion.21), kind=kCustom, calls=%fused_computation.2.clone | custom fusion | bytes 2105344 | tf_op jit(solution)/shard_map/jit(_take)/gather | solution.py:141
  36.6 9.0 %gather_fusion.1 = bf16[2048,256]{1,0:T(8,128)(2,1)} fusion(bf16[2048,256]{1,0:T(8,128)(2,1)S(1)} %copy-done, s32[2048]{0:T(1024)S(1)} %fusion.21), kind=kCustom, calls=%fused_computation.1.clone | custom fusion | bytes 2105344 | tf_op jit(solution)/shard_map/jit(_take)/gather | solution.py:140
  45.6 9.0 %gather_fusion = bf16[2048,256]{1,0:T(8,128)(2,1)} fusion(bf16[2048,256]{1,0:T(8,128)(2,1)S(1)} %copy-done.2, s32[2048]{0:T(1024)S(1)} %fusion.21), kind=kCustom, calls=%fused_computation.clone | custom fusion | bytes 2105344 | tf_op jit(solution)/shard_map/jit(_take)/gather | solution.py:139
  54.6 3.1 %broadcast_select_fusion.2 = (bf16[2048,256]{1,0:T(8,128)(2,1)S(1)}, bf16[2048,256]{1,0:T(8,128)(2,1)}, bf16[2048,256]{1,0:T(8,128)(2,1)}) fusion(bf16[2048,256]{1,0:T(8,128)(2,1)} %gather_fusion, pred[2048]{0:T(1024)(128)(4,1)S(1)} %compare_and_fusion.1, bf16[2048,256]{1,0:T(8,128)(2,1)} %gather_fusion.1, bf16[2048,256]{1,0:T(8,128)(2,1)} %gather_fusion.2), kind=kLoop, calls=%fused_computation.49 | loop fusion | flops 1572864 | bytes 6293504 | tf_op jit(solution)/shard_map/jit(_take)/select_n | solution.py:139
  57.7 1.8 reduce_sum.160
  59.5 1.4 multiply_reduce_fusion.10
  60.9 2.0 pad_maximum_fusion.2
  63.4 9.8 %all-to-all-start.1 = ((f32[32,1,3]{2,1,0:T(1,128)}), f32[32,1,3]{2,1,0:T(1,128)}, u32[]{:S(2)}, u32[]{:S(2)}) async-start(f32[32,1,3]{2,1,0:T(1,128)} %broadcast_in_dim.21), calls=%async_computation.1 | async-start | bytes 32768 | tf_op jit(solution)/shard_map/all_to_all | solution.py:40
  73.3 3.1 %pad_maximum_fusion = bf16[32,6,32,256]{3,2,1,0:T(8,128)(2,1)} fusion(bf16[32,2,32,256]{3,2,1,0:T(8,128)(2,1)} %bitcast.176, bf16[32,2,32,256]{3,2,1,0:T(8,128)(2,1)} %bitcast.175, bf16[32,2,32,256]{3,2,1,0:T(8,128)(2,1)S(1)} %bitcast.174), kind=kLoop, calls=%fused_computation.17 | loop fusion | flops 3145728 | bytes 6291456 | tf_op jit(solution)/shard_map/concatenate | solution.py:14
  76.4 6.2 %all-to-all-done.1 = f32[32,1,3]{2,1,0:T(1,128)} async-done(((f32[32,1,3]{2,1,0:T(1,128)}), f32[32,1,3]{2,1,0:T(1,128)}, u32[]{:S(2)}, u32[]{:S(2)}) %all-to-all-start.1) | async-done | bytes 416 | tf_op jit(solution)/shard_map/all_to_all | solution.py:40
  82.5 5.0 %all-to-all-start.3 = ((bf16[32,6,32,256]{3,2,1,0:T(8,128)(2,1)}), bf16[32,6,32,256]{3,2,1,0:T(8,128)(2,1)}, u32[]{:S(2)}, u32[]{:S(2)}) async-start(bf16[32,6,32,256]{3,2,1,0:T(8,128)(2,1)} %pad_maximum_fusion), calls=%async_computation.3 | async-start | bytes 6291456 | tf_op jit(solution)/shard_map/all_to_all | solution.py:15
  87.6 0.7 multiply_reduce_fusion.2
  89.0 0.7 multiply_reduce_fusion.3
  90.2 0.7 multiply_reduce_fusion.4
  91.7 0.8 reduce_sum.167
  92.5 0.6 fusion.29
  95.6 95.0 %all_gather.3 = bf16[3,256,256]{2,1,0:T(8,128)(2,1)S(1)} all-gather(bf16[3,8,256]{2,1,0:T(8,128)(2,1)S(1)} %pad_maximum_fusion.1), channel_id=1, replica_groups=mesh['cam'=32,'head'=16] {'cam'}, dimensions={1}, use_global_device_ids=true | all-gather | bytes 405504 | tf_op jit(solution)/shard_map/all_gather | solution.py:61
  190.6 1.9 convolution_bitcast_fusion.2
  192.4 3.9 %multiply_reduce_fusion.1 = (f32[2048]{0:T(1024)S(1)}, f32[2048,256]{0,1:T(8,128)}) fusion(bf16[2048,256]{1,0:T(8,128)(2,1)S(1)} %copy-done.2, f32[2048,1,256]{0,2,1:T(8,128)} %convolution_bitcast_fusion.2, bf16[3,256,256]{2,1,0:T(8,128)(2,1)S(1)} %all_gather.3), kind=kOutput, calls=%fused_computation.28 | convolution fusion | flops 541063168 | bytes 5513216 | tf_op jit(solution)/shard_map/nhk,hdk->nhd/dot_general | solution.py:175
  196.4 0.7 broadcast_in_dim.22
  197.1 10.2 %all-to-all-start.2 = ((f32[16,1,2048]{2,1,0:T(1,128)}), f32[16,1,2048]{2,1,0:T(1,128)S(1)}, u32[]{:S(2)}, u32[]{:S(2)}) async-start(f32[16,1,2048]{2,1,0:T(1,128)} %broadcast_in_dim.22), calls=%async_computation.2 | async-start | bytes 262144 | tf_op jit(solution)/shard_map/all_to_all | solution.py:40
  207.3 3.7 %slice_bitcast_fusion = (bf16[2,32,32,256]{3,2,0,1:T(8,128)(2,1)S(1)}, bf16[2,32,32,256]{3,2,0,1:T(8,128)(2,1)}, bf16[2,32,32,256]{3,2,0,1:T(8,128)(2,1)}) fusion(bf16[32,6,32,256]{3,2,1,0:T(8,128)(2,1)} %all-to-all-done.3), kind=kLoop, calls=%fused_computation.37 | loop fusion | bytes 6291456 | tf_op jit(solution)/shard_map/transpose | solution.py:125
  211.0 11.8 %while.10 = (s32[]{:T(128)}, bf16[2,32,32,256]{3,2,0,1:T(8,128)(2,1)}, bf16[2,32,32,256]{3,2,0,1:T(8,128)(2,1)}, bf16[2,32,32,256]{3,2,0,1:T(8,128)(2,1)}, bf16[2,32,32,256]{3,2,0,1:T(8,128)(2,1)S(1)}, /*index=5*/s32[]{:T(128)}) while((s32[]{:T(128)}, bf16[2,32,32,256]{3,2,0,1:T(8,128)(2,1)}, bf16[2,32,32,256]{3,2,0,1:T(8,128)(2,1)}, ...), condition=%wide.region_20.22_spmd, body=%wide.region_17.21_spmd.sunk | while | flops 1083439104 | bytes 19943512 | solution.py:128
  211.0 1.1 constant_dynamic-slice_fusion.5
  212.1 1.1 constant_dynamic-slice_fusion.6
  213.2 0.8 multiply_reduce_fusion.12
  214.0 0.7 fusion.45
  214.7 1.1 fusion.46
  216.1 0.8 constant_dynamic-update-slice_fusion.2
  216.9 1.1 constant_dynamic-slice_fusion.5
  218.0 1.1 constant_dynamic-slice_fusion.6
  219.1 0.8 multiply_reduce_fusion.12
  219.9 0.7 fusion.45
  220.6 1.1 fusion.46
  221.9 0.8 constant_dynamic-update-slice_fusion.2
  222.8 9.6 %all-to-all-start.4 = ((bf16[32,2,32,256]{3,2,1,0:T(8,128)(2,1)}), bf16[32,2,32,256]{3,2,1,0:T(8,128)(2,1)S(1)}, u32[]{:S(2)}, u32[]{:S(2)}) async-start(bf16[32,2,32,256]{3,2,1,0:T(8,128)(2,1)} %bitcast.177), calls=%async_computation.4 | async-start | bytes 2097152 | tf_op jit(solution)/shard_map/all_to_all | solution.py:143
  232.5 27.9 %all-to-all-done.4 = bf16[32,2,32,256]{3,2,1,0:T(8,128)(2,1)S(1)} async-done(((bf16[32,2,32,256]{3,2,1,0:T(8,128)(2,1)}), bf16[32,2,32,256]{3,2,1,0:T(8,128)(2,1)S(1)}, u32[]{:S(2)}, u32[]{:S(2)}) %all-to-all-start.4) | async-done | bytes 1048608 | tf_op jit(solution)/shard_map/all_to_all | solution.py:143
  260.4 7.5 %gather_fusion.3 = bf16[2048,256]{1,0:T(8,128)(2,1)S(1)} fusion(bf16[2048,256]{1,0:T(8,128)(2,1)S(1)} %bitcast.169, s32[2048]{0:T(1024)S(1)} %fusion.22), kind=kCustom, calls=%fused_computation.3.clone | custom fusion | bytes 2105344 | tf_op jit(solution)/shard_map/jit(_take)/gather | solution.py:146
  268.6 2.1 add_convert_fusion
  270.7 1.3 copy.70
  (44 shorter events, 4.6 us)
Async XLA Ops:
  0.0 2.3 copy-start
  0.0 2.3 copy-start.3
  2.3 0.9 copy-start.4
  3.2 0.9 copy-start.5
  7.2 12.3 %copy-start.7 = (s32[1,2048]{1,0:T(1,128)S(1)}, s32[1,2048]{1,0:T(1,128)}, u32[]{:S(2)}) copy-start(s32[1,2048]{1,0:T(1,128)} %param.21) | copy-start | bytes 24580
  7.2 20.4 %copy-start.1 = (bf16[2048,256]{1,0:T(8,128)(2,1)S(1)}, bf16[2048,256]{1,0:T(8,128)(2,1)}, u32[]{:S(2)}) copy-start(bf16[2048,256]{1,0:T(8,128)(2,1)} %param.15) | copy-start | bytes 3145732
  8.2 49.5 %all-to-all-start = ((f32[32,3,8,256]{3,2,1,0:T(8,128)}), f32[32,3,8,256]{3,2,1,0:T(8,128)}, u32[]{:S(2)}, u32[]{:S(2)}) async-start(f32[32,3,8,256]{3,2,1,0:T(8,128)} %copy.62), calls=%async_computation | async-start | bytes 1572864 | tf_op jit(solution)/shard_map/all_to_all | solution.py:27
  36.6 9.0 %copy-start.2 = (bf16[2048,256]{1,0:T(8,128)(2,1)S(1)}, bf16[2048,256]{1,0:T(8,128)(2,1)}, u32[]{:S(2)}) copy-start(bf16[2048,256]{1,0:T(8,128)(2,1)} %param.13) | copy-start | bytes 3145732
  63.4 19.1 %all-to-all-start.1 = ((f32[32,1,3]{2,1,0:T(1,128)}), f32[32,1,3]{2,1,0:T(1,128)}, u32[]{:S(2)}, u32[]{:S(2)}) async-start(f32[32,1,3]{2,1,0:T(1,128)} %broadcast_in_dim.21), calls=%async_computation.1 | async-start | bytes 32768 | tf_op jit(solution)/shard_map/all_to_all | solution.py:40
  76.3 18.8 %copy-start.6 = (f32[3,8,256]{2,1,0:T(8,128)S(1)}, f32[3,8,256]{2,1,0:T(8,128)}, u32[]{:S(2)}) copy-start(f32[3,8,256]{2,1,0:T(8,128)} %reduce_sum.160) | copy-start | bytes 73732
  82.5 113.9 %all-to-all-start.3 = ((bf16[32,6,32,256]{3,2,1,0:T(8,128)(2,1)}), bf16[32,6,32,256]{3,2,1,0:T(8,128)(2,1)}, u32[]{:S(2)}, u32[]{:S(2)}) async-start(bf16[32,6,32,256]{3,2,1,0:T(8,128)(2,1)} %pad_maximum_fusion), calls=%async_computation.3 | async-start | bytes 6291456 | tf_op jit(solution)/shard_map/all_to_all | solution.py:15
  197.1 25.7 %all-to-all-start.2 = ((f32[16,1,2048]{2,1,0:T(1,128)}), f32[16,1,2048]{2,1,0:T(1,128)S(1)}, u32[]{:S(2)}, u32[]{:S(2)}) async-start(f32[16,1,2048]{2,1,0:T(1,128)} %broadcast_in_dim.22), calls=%async_computation.2 | async-start | bytes 262144 | tf_op jit(solution)/shard_map/all_to_all | solution.py:40
  222.8 37.7 %all-to-all-start.4 = ((bf16[32,2,32,256]{3,2,1,0:T(8,128)(2,1)}), bf16[32,2,32,256]{3,2,1,0:T(8,128)(2,1)S(1)}, u32[]{:S(2)}, u32[]{:S(2)}) async-start(bf16[32,2,32,256]{3,2,1,0:T(8,128)(2,1)} %bitcast.177), calls=%async_computation.4 | async-start | bytes 2097152 | tf_op jit(solution)/shard_map/all_to_all | solution.py:143
  267.9 0.7 copy-start.8
where the time goes:
time: 274 us; the launch traced here: 272 us
  blocking collectives  95 us (35%)
  local copies, waits for them, and re-layouts  60 us (22%)
  starting transfers between devices  45.9 us (17%)
  waiting for transfers between devices  34.1 us (12%)
  other arithmetic  19.1 us (7%)
  matrix products  13.5 us (5%)
  between operations  4.36 us (2%)
    all_gather x1, blocking collectives, in_one_piece_2(): lax.all_gather(both, axis, axis=dim, tiled=True)  95 us
    all_to_all x1, waiting for transfers between devices, per_device(): lax.all_to_all(attend(arrived, local, head_size), 'cam', split_axis=0, co...  27.9 us
    all_to_all x2, starting transfers between devices, sent_to_all(): lax.all_to_all(jnp.broadcast_to(shard[None], (devices, *shard.shape)), ax...  20 us
    all_to_all x1, starting transfers between devices, sum_at_owner(): lax.all_to_all(split_up(shard, dim, devices), axis, 0, 0, tiled=True)  11.3 us
    all_to_all x1, starting transfers between devices, per_device(): lax.all_to_all(attend(arrived, local, head_size), 'cam', split_axis=0, co...  9.57 us
    gather x1, local copies, waits for them, and re-layouts, per_device(): jnp.take(queries, inverse, axis=0).reshape(cams, owned, PATCHES, width)  9.05 us
    gather x1, local copies, waits for them, and re-layouts, per_device(): jnp.take(values, inverse, axis=0).reshape(cams, owned, PATCHES, width)  9 us
    gather x1, local copies, waits for them, and re-layouts, per_device(): jnp.take(keys, inverse, axis=0).reshape(cams, owned, PATCHES, width)  8.98 us
  transfers between devices with their start and end apart: 5, of which 2 were waited for; matrix products, arithmetic and copies ran while one was open for 24% of the time, Pallas kernels for 0%

commit v1 on v0

v1 whole, which is shorter than its diff:
```python
import functools
import jax
import jax.numpy as jnp
from jax import lax
from jax.experimental import pallas as pl
from jax.experimental.pallas import tpu as pltpu
from jax.sharding import PartitionSpec as P

PATCHES = 32
EPSILON = 1e-06
GROUP = 8
PLANE = 4
MESH = pl.DeviceIdType.MESH
F32 = jnp.float32
BF16 = jnp.bfloat16


def nt(a, b):
    return lax.dot_general(a, b, (((1,), (1,)), ((), ())), preferred_element_type=F32)


def nn(a, b):
    return jnp.dot(a, b, preferred_element_type=F32)


def column_of(row):
    return jnp.transpose(jnp.broadcast_to(row, (128, 128)))


def drain(ref, sem):
    pltpu.make_async_copy(ref, ref, sem).wait()


def renewed(weight, grad):
    wf = weight.astype(F32)
    scale = jnp.sqrt(jnp.mean(wf * wf)) / jnp.sqrt(jnp.mean(grad * grad) + EPSILON)
    moved = wf - scale * grad
    ratio = jnp.sqrt(jnp.sum(wf * wf, axis=1, keepdims=True)) / jnp.sqrt(
        jnp.sum(moved * moved, axis=1, keepdims=True) + EPSILON
    )
    return (moved * ratio).astype(BF16)


def layer(
    cams, heads,
    q_ref, k_ref, v_ref, rates_ref, w1_ref, w3_ref, w2_ref, gain_ref, order_ref,
    out_ref,
    sbuf, rbuf, obuf, ret, gbuf, gall, plane_in, line_in, line_own, u_buf, y_buf,
    rcol, ocol, sq_own, sq_in,
    bulk_send, bulk_recv, back_send, back_recv,
    g_send, g_recv, sq_send, sq_recv,
):
    count, width = q_ref.shape
    lines = cams // PLANE
    blocks = cams // GROUP
    rows = GROUP * PATCHES
    frame_rows = cams * PATCHES
    hid = w1_ref.shape[0]
    plane_rows = hid // PLANE
    line_rows = plane_rows // lines
    cam = lax.axis_index("cam")
    head = lax.axis_index("head")
    line, place = cam // PLANE, cam % PLANE

    barrier = pltpu.get_barrier_semaphore()

    def greet_cam(o, c):
        pl.semaphore_signal(
            barrier, inc=1, device_id=((cam + o) % cams, head), device_id_type=MESH
        )
        return c

    def greet_head(o, c):
        pl.semaphore_signal(
            barrier, inc=1, device_id=(cam, (head + o) % heads), device_id_type=MESH
        )
        return c

    lax.fori_loop(1, cams, greet_cam, 0)
    lax.fori_loop(1, heads, greet_head, 0)

    def block_at(turn):
        return (cam // GROUP + turn) % blocks

    def sort_block(frame, turn):
        blk = block_at(turn)
        first = frame * frame_rows + blk * rows
        slot = lax.broadcasted_iota(jnp.int32, (rows, count), 0) + first
        pick = jnp.where(slot == order_ref[...], 1.0, 0.0).astype(BF16)
        for a, ref in enumerate((q_ref, k_ref, v_ref)):
            got = nn(pick, ref[...]).astype(BF16).reshape(GROUP, PATCHES, width)
            sbuf[frame, pl.ds(blk * GROUP, GROUP), a] = got

    def send_block(frame, turn):
        blk = block_at(turn)

        def one(j, c):
            dest = blk * GROUP + (cam + j) % GROUP
            pltpu.make_async_remote_copy(
                src_ref=sbuf.at[frame, dest],
                dst_ref=rbuf.at[frame, cam],
                send_sem=bulk_send.at[frame],
                recv_sem=bulk_recv.at[frame],
                device_id=(dest, head),
                device_id_type=MESH,
            ).start()
            return c

        if turn == 0:
            pltpu.make_async_copy(
                sbuf.at[frame, cam], rbuf.at[frame, cam], bulk_recv.at[frame]
            ).start()
        lax.fori_loop(1 if turn == 0 else 0, GROUP, one, 0)

    def attend_block(frame, turn):
        blk = block_at(turn)
        query = rbuf[frame, pl.ds(blk * GROUP, GROUP), 0].reshape(rows, width)
        key = rbuf[frame, :, 1].reshape(frame_rows, width)
        value = rbuf[frame, :, 2].reshape(frame_rows, width)
        scores = nt(query, key) * (width ** (-0.5))
        expo = jnp.exp(scores - jnp.max(scores, axis=1, keepdims=True))
        probs = (expo * (1.0 / jnp.sum(expo, axis=1, keepdims=True))).astype(BF16)
        got = nn(probs, value).astype(BF16).reshape(GROUP, PATCHES, width)
        obuf[frame, pl.ds(blk * GROUP, GROUP)] = got

    def return_block(frame, turn):
        blk = block_at(turn)

        def one(j, c):
            dest = blk * GROUP + (cam + j) % GROUP
            pltpu.make_async_remote_copy(
                src_ref=obuf.at[frame, dest],
                dst_ref=ret.at[frame, cam],
                send_sem=back_send.at[frame],
                recv_sem=back_recv.at[frame],
                device_id=(dest, head),
                device_id_type=MESH,
            ).start()
            return c

        if turn == 0:
            pltpu.make_async_copy(
                obuf.at[frame, cam], ret.at[frame, cam], back_recv.at[frame]
            ).start()
        lax.fori_loop(1 if turn == 0 else 0, GROUP, one, 0)

    turns = [t for t in (2, 1, 3, 0) if t < blocks]
    early, late = turns[: blocks // 2], turns[blocks // 2 :]

    def columns(b, c):
        lanes = pl.ds(pl.multiple_of(b * 128, 128), 128)
        here = pl.ds(pl.multiple_of(b * 128, 128), 128)
        rcol[here] = column_of(rates_ref[:, lanes])
        ocol[here] = column_of(order_ref[:, lanes].astype(F32))
        return c

    def grad_step(i, c):
        step = 512
        here = pl.ds(pl.multiple_of(i * step, step), step)
        key, val = k_ref[here], v_ref[here].astype(F32)
        rate = rcol[here]
        err = (-jnp.concatenate([rate, rate], axis=1) * val).astype(BF16)
        a1, a3 = nt(w1_ref[...], key), nt(w3_ref[...], key)
        s = jax.nn.sigmoid(a1)
        act = (a1 * s * a3).astype(BF16)
        back = nt(u_buf[0], err)
        b1 = (back * a3 * s * (1.0 + a1 * (1.0 - s))).astype(BF16)
        b3 = (back * a1 * s).astype(BF16)
        gbuf[0] += nn(b1, key)
        gbuf[1] += nn(b3, key)
        gbuf[2] += nn(act, err)
        return c

    def plane_peer(o):
        return (line * PLANE + (place + o) % PLANE, head)

    def line_peer(o):
        return (((line + o) % lines) * PLANE + place, head)

    def stage(n, src, dst, peer):
        pltpu.make_async_remote_copy(
            src_ref=src, dst_ref=dst, send_sem=g_send.at[n], recv_sem=g_recv.at[n],
            device_id=peer, device_id_type=MESH,
        ).start()

    sort_block(0, early[0] if early else turns[0])
    pl.semaphore_wait(barrier, cams - 1 + heads - 1)
    send_block(0, early[0] if early else turns[0])
    for t in early[1:]:
        sort_block(0, t)
        send_block(0, t)

    lax.fori_loop(0, count // 128, columns, 0)
    u_buf[0] = jnp.transpose(w2_ref[...].astype(F32)).astype(BF16)
    gbuf[...] = jnp.zeros_like(gbuf)
    lax.fori_loop(0, count // 512, grad_step, 0)
    for o in range(1, PLANE):
        theirs = pl.ds(((place + o) % PLANE) * plane_rows, plane_rows)
        stage(0, gbuf.at[:, theirs], plane_in.at[o - 1], plane_peer(o))
    for t in (late if early else late[1:]):
        sort_block(0, t)
        send_block(0, t)
    drain(plane_in, g_recv.at[0])
    drain(plane_in, g_send.at[0])
    mine = pl.ds(place * plane_rows, plane_rows)
    gbuf[:, mine] += plane_in[0] + plane_in[1] + plane_in[2]

    sort_block(1, turns[0])
    for o in range(1, lines):
        theirs = pl.ds(place * plane_rows + ((line + o) % lines) * line_rows, line_rows)
        stage(1, gbuf.at[:, theirs], line_in.at[o - 1], line_peer(o))
    send_block(1, turns[0])
    for t in turns[1:2]:
        sort_block(1, t)
        send_block(1, t)
    drain(line_in, g_recv.at[1])
    drain(line_in, g_send.at[1])
    own = pl.ds(place * plane_rows + line * line_rows, line_rows)
    total = gbuf[:, own]
    for o in range(1, lines):
        total = total + line_in[o - 1]
    line_own[...] = total
    gall[:, own] = total
    for t in turns[2:3]:
        sort_block(1, t)
    for o in range(1, lines):
        stage(2, line_own, gall.at[:, own], line_peer(o))
    for t in turns[2:3]:
        send_block(1, t)
    for t in turns[3:]:
        sort_block(1, t)
    drain(line_in, g_recv.at[2])
    drain(line_in, g_send.at[2])
    for o in range(1, PLANE):
        stage(3, gall.at[:, mine], gall.at[:, mine], plane_peer(o))
    for t in turns[3:]:
        send_block(1, t)
    drain(plane_in, g_recv.at[3])
    drain(plane_in, g_send.at[3])

    u_buf[0] = renewed(w1_ref[...], gall[0])
    u_buf[1] = renewed(w3_ref[...], gall[1])
    u_buf[2] = renewed(w2_ref[...], jnp.transpose(gall[2]))

    def readout(i, c):
        step = 256
        here = pl.ds(pl.multiple_of(i * step, step), step)
        query = q_ref[here]
        q1, q3 = nt(query, u_buf[0]), nt(query, u_buf[1])
        act = (q1 * jax.nn.sigmoid(q1) * q3).astype(BF16)
        y = nt(act, u_buf[2])
        y_buf[here] = y
        half = y[:, :128] * y[:, :128] + y[:, 128:] * y[:, 128:]
        for b in range(step // 128):
            part = jnp.sum(jnp.transpose(half[b * 128 : (b + 1) * 128]), axis=0, keepdims=True)
            sq_own[pl.ds(i * (step // 128) + b, 1)] = part
        return c

    lax.fori_loop(0, count // 256, readout, 0)

    def send_sq(o, c):
        pltpu.make_async_remote_copy(
            src_ref=sq_own, dst_ref=sq_in.at[o - 1], send_sem=sq_send, recv_sem=sq_recv,
            device_id=(cam, (head + o) % heads), device_id_type=MESH,
        ).start()
        return c

    drain(rbuf.at[0], bulk_recv.at[0])
    attend_block(0, turns[0])
    lax.fori_loop(1, heads, send_sq, 0)
    for a, b in zip(turns[1:], turns[:-1]):
        attend_block(0, a)
        return_block(0, b)
    drain(rbuf.at[1], bulk_recv.at[1])
    attend_block(1, turns[0])
    return_block(0, turns[-1])
    for a, b in zip(turns[1:], turns[:-1]):
        attend_block(1, a)
        return_block(1, b)

    drain(sq_in, sq_recv)
    square = sq_own[...]
    for o in range(1, heads):
        square = square + sq_in[o - 1]
    sq_own_inv = 1.0 / jnp.sqrt(square / (width * heads) + EPSILON)
    drain(sq_in, sq_send)
    return_block(1, turns[-1])
    sq_own[...] = sq_own_inv

    def scaled(b, c):
        here = pl.ds(pl.multiple_of(b * 128, 128), 128)
        inv = column_of(sq_own[pl.ds(b, 1)])
        y_buf[here] = y_buf[here] * jnp.concatenate([inv, inv], axis=1) * gain_ref[...]
        return c

    lax.fori_loop(0, count // 128, scaled, 0)

    def taken(frame, here, step):
        at = ocol[here]
        lane = lax.broadcasted_iota(jnp.int32, (step, 128), 1).astype(F32)
        pick = jnp.concatenate(
            [
                jnp.where(at == lane + float(frame * frame_rows + b * 128), 1.0, 0.0).astype(BF16)
                for b in range(frame_rows // 128)
            ],
            axis=1,
        )
        return nn(pick, ret[frame].reshape(frame_rows, width))

    drain(ret.at[0], back_recv.at[0])

    def first_half(i, c):
        here = pl.ds(pl.multiple_of(i * 256, 256), 256)
        y_buf[here] += taken(0, here, 256)
        return c

    lax.fori_loop(0, count // 256, first_half, 0)
    drain(ret.at[1], back_recv.at[1])

    def second_half(i, c):
        here = pl.ds(pl.multiple_of(i * 256, 256), 256)
        out_ref[here] = (y_buf[here] + taken(1, here, 256)).astype(BF16)
        return c

    lax.fori_loop(0, count // 256, second_half, 0)
    for frame in range(2):
        drain(sbuf.at[frame, pl.ds(0, cams - 1)], bulk_send.at[frame])
        drain(obuf.at[frame, pl.ds(0, cams - 1)], back_send.at[frame])


def per_device(cams, heads, queries, keys, values, rates, w_one, w_three, w_two, gain, order):
    count, width = queries.shape
    hid = w_one.shape[1]
    plane_rows = hid // PLANE
    lines = cams // PLANE
    line_rows = plane_rows // lines
    dma = pltpu.SemaphoreType.DMA
    vmem = pl.BlockSpec(memory_space=pltpu.VMEM)
    return pl.pallas_call(
        functools.partial(layer, cams, heads),
        out_shape=jax.ShapeDtypeStruct((count, width), BF16),
        in_specs=[vmem] * 9,
        out_specs=vmem,
        scratch_shapes=[
            pltpu.VMEM((2, cams, 3, PATCHES, width), BF16),
            pltpu.VMEM((2, cams, 3, PATCHES, width), BF16),
            pltpu.VMEM((2, cams, PATCHES, width), BF16),
            pltpu.VMEM((2, cams, PATCHES, width), BF16),
            pltpu.VMEM((3, hid, width), F32),
            pltpu.VMEM((3, hid, width), F32),
            pltpu.VMEM((PLANE - 1, 3, plane_rows, width), F32),
            pltpu.VMEM((lines - 1, 3, line_rows, width), F32),
            pltpu.VMEM((3, line_rows, width), F32),
            pltpu.VMEM((3, hid, width), BF16),
            pltpu.VMEM((count, width), F32),
            pltpu.VMEM((count, 128), F32),
            pltpu.VMEM((count, 128), F32),
            pltpu.VMEM((count // 128, 128), F32),
            pltpu.VMEM((heads - 1, count // 128, 128), F32),
            dma((2,)),
            dma((2,)),
            dma((2,)),
            dma((2,)),
            dma((4,)),
            dma((4,)),
            dma,
            dma,
        ],
        compiler_params=pltpu.CompilerParams(
            collective_id=0, has_side_effects=True, vmem_limit_bytes=60 * 1024 * 1024
        ),
        name="layer",
    )(
        queries, keys, values, rates.reshape(1, count),
        w_one[0], w_three[0], w_two[0], gain.reshape(1, width), order,
    )


def solution(mesh):
    in_specs = (
        P("cam", "head"),
        P("cam", "head"),
        P("cam", "head"),
        P("cam", "head"),
        P("head", None, None),
        P("head", None, None),
        P("head", None, None),
        P("head"),
        P("cam", None),
    )
    step = functools.partial(per_device, mesh.shape["cam"], mesh.shape["head"])
    return jax.shard_map(
        step, mesh=mesh, in_specs=in_specs, out_specs=P("cam", "head"), check_vma=False
    )
```

time: 274 us -> 145 us (0.53)
  Pallas kernels: 0 us -> 142 us
  blocking collectives: 95 us -> 0 us
  local copies, waits for them, and re-layouts: 60 us -> 2.26 us
  starting transfers between devices: 45.9 us -> 0 us
  waiting for transfers between devices: 34.1 us -> 0 us
  other arithmetic: 19.1 us -> 0 us
  matrix products: 13.5 us -> 0 us
  between operations: 4.36 us -> 0.01 us
    pallas_call x0 -> x1, Pallas kernels: none -> 142 us  [per_device(): pl.pallas_call(functools.partial(layer, cams, heads), out_shape=jax.Shape...]
    all_gather x1 -> x0, blocking collectives: 95 us -> none  [in_one_piece_2(): lax.all_gather(both, axis, axis=dim, tiled=True)]
    all_to_all x5 -> x0, starting transfers between devices: 45.9 us -> none  [the longest x2 20 us: sent_to_all(): lax.all_to_all(jnp.broadcast_to(shard[None], (devices, *shard.shape)), ax...]
    gather x5 -> x0, local copies, waits for them, and re-layouts: 35.2 us -> none  [the longest x1 9.05 us: per_device(): jnp.take(queries, inverse, axis=0).reshape(cams, owned, PATCHES, width)]
    all_to_all x5 -> x0, waiting for transfers between devices: 34.1 us -> none  [the longest x1 27.9 us: per_device(): lax.all_to_all(attend(arrived, local, head_size), 'cam', split_axis=0, co...]
    dot_general x12 -> x0, matrix products: 13.5 us -> none  [the longest x1 3.94 us: per_device(): jnp.einsum('nhk,hdk->nhd', q_active, new_second, preferred_element_type=j...]
    scatter x1 -> x0, local copies, waits for them, and re-layouts: 8.05 us -> none  [per_device(): jnp.zeros((count,), jnp.int32).at[slots]]
    reduce_sum x11 -> x0, other arithmetic: 7.94 us -> none  [the longest x3 2.1 us: weight_scale(): return jnp.sqrt(jnp.mean(wf * wf, axis=(1, 2)))]
  transfers between devices with their start and end apart: 5 -> 0, of which waited for: 2 -> 0; matrix products, arithmetic and copies ran while one was open for 24% -> 0% of each run, Pallas kernels for 0% -> 0%
where the time goes in v1:
time: 145 us
  Pallas kernels  142 us (98%)
  local copies, waits for them, and re-layouts  2.26 us (2%)
    pallas_call x1, Pallas kernels, per_device(): pl.pallas_call(functools.partial(layer, cams, heads), out_shape=jax.Shape...  142 us

profile of v1, /device:TPU:1, one launch (start us, length us, event | category | flops | bytes accessed | tf_op | source)
XLA Modules:
  0.0 144.7 jit_solution(12326277789856349636)
XLA Ops:
  0.0 142.4 %layer.1 = bf16[2048,256]{1,0:T(8,128)(2,1)} custom-call(bf16[2048,256]{1,0:T(8,128)(2,1)} %q_ref.1, bf16[2048,256]{1,0:T(8,128)(2,1)} %k_ref.1, bf16[2048,256]{1,0:T(8,128)(2,1)} %v_ref.1, f32[1,2048]{1,0:T(1,128)} %bitcast.8, bf16[256,256]{1,0:T(8,128)(2,1)} %bitcast.5, bf16[256,256]{1,0:T(8,128)(2,1)} %bitcast.6, bf16[256,256]{1,0:T(8,128)(2,1)} %bitcast.7, ...), custom_call_target="tpu_custom_call" | custom-call | tf_op jit(solution)/shard_map/layer/pallas_call | solution.py:339
  142.4 2.3 %copy.11 = bf16[2048,256]{1,0:T(8,128)(2,1)} copy(bf16[2048,256]{1,0:T(8,128)(2,1)} %layer.1) | data formatting | bytes 2097152

commit v2 on v1

--- a/solution.py
+++ b/solution.py
@@ -45,7 +45,7 @@
     cams, heads,
     q_ref, k_ref, v_ref, rates_ref, w1_ref, w3_ref, w2_ref, gain_ref, order_ref,
     out_ref,
-    sbuf, rbuf, obuf, ret, gbuf, gall, plane_in, line_in, line_own, u_buf, y_buf,
+    sbuf, rbuf, obuf, ret, gbuf, gall, plane_in, line_in, u_buf, y_buf,
     rcol, ocol, sq_own, sq_in,
     bulk_send, bulk_recv, back_send, back_recv,
     g_send, g_recv, sq_send, sq_recv,
@@ -132,7 +132,7 @@
                 src_ref=obuf.at[frame, dest],
                 dst_ref=ret.at[frame, cam],
                 send_sem=back_send.at[frame],
-                recv_sem=back_recv.at[frame],
+                recv_sem=back_recv.at[frame, turn],
                 device_id=(dest, head),
                 device_id_type=MESH,
             ).start()
@@ -140,12 +140,11 @@
 
         if turn == 0:
             pltpu.make_async_copy(
-                obuf.at[frame, cam], ret.at[frame, cam], back_recv.at[frame]
+                obuf.at[frame, cam], ret.at[frame, cam], back_recv.at[frame, turn]
             ).start()
         lax.fori_loop(1 if turn == 0 else 0, GROUP, one, 0)
 
     turns = [t for t in (2, 1, 3, 0) if t < blocks]
-    early, late = turns[: blocks // 2], turns[blocks // 2 :]
 
     def columns(b, c):
         lanes = pl.ds(pl.multiple_of(b * 128, 128), 128)
@@ -183,21 +182,18 @@
             device_id=peer, device_id_type=MESH,
         ).start()
 
-    sort_block(0, early[0] if early else turns[0])
-    pl.semaphore_wait(barrier, cams - 1 + heads - 1)
-    send_block(0, early[0] if early else turns[0])
-    for t in early[1:]:
-        sort_block(0, t)
-        send_block(0, t)
-
     lax.fori_loop(0, count // 128, columns, 0)
     u_buf[0] = jnp.transpose(w2_ref[...].astype(F32)).astype(BF16)
     gbuf[...] = jnp.zeros_like(gbuf)
     lax.fori_loop(0, count // 512, grad_step, 0)
+    sort_block(0, turns[0])
+    pl.semaphore_wait(barrier, cams - 1 + heads - 1)
+
     for o in range(1, PLANE):
         theirs = pl.ds(((place + o) % PLANE) * plane_rows, plane_rows)
         stage(0, gbuf.at[:, theirs], plane_in.at[o - 1], plane_peer(o))
-    for t in (late if early else late[1:]):
+    send_block(0, turns[0])
+    for t in turns[1:2]:
         sort_block(0, t)
         send_block(0, t)
     drain(plane_in, g_recv.at[0])
@@ -205,36 +201,45 @@
     mine = pl.ds(place * plane_rows, plane_rows)
     gbuf[:, mine] += plane_in[0] + plane_in[1] + plane_in[2]
 
-    sort_block(1, turns[0])
+    for t in turns[2:3]:
+        sort_block(0, t)
     for o in range(1, lines):
         theirs = pl.ds(place * plane_rows + ((line + o) % lines) * line_rows, line_rows)
         stage(1, gbuf.at[:, theirs], line_in.at[o - 1], line_peer(o))
-    send_block(1, turns[0])
-    for t in turns[1:2]:
-        sort_block(1, t)
-        send_block(1, t)
+    for t in turns[2:3]:
+        send_block(0, t)
+    for t in turns[3:]:
+        sort_block(0, t)
+        send_block(0, t)
     drain(line_in, g_recv.at[1])
     drain(line_in, g_send.at[1])
     own = pl.ds(place * plane_rows + line * line_rows, line_rows)
     total = gbuf[:, own]
     for o in range(1, lines):
         total = total + line_in[o - 1]
-    line_own[...] = total
     gall[:, own] = total
-    for t in turns[2:3]:
+    sort_block(1, turns[0])
+
+    for o in range(1, lines):
+        stage(2, gall.at[:, own], gall.at[:, own], line_peer(o))
+    send_block(1, turns[0])
+    for t in turns[1:2]:
         sort_block(1, t)
-    for o in range(1, lines):
-        stage(2, line_own, gall.at[:, own], line_peer(o))
-    for t in turns[2:3]:
         send_block(1, t)
-    for t in turns[3:]:
-        sort_block(1, t)
     drain(line_in, g_recv.at[2])
     drain(line_in, g_send.at[2])
     for o in range(1, PLANE):
         stage(3, gall.at[:, mine], gall.at[:, mine], plane_peer(o))
-    for t in turns[3:]:
+    for t in turns[2:]:
+        sort_block(1, t)
         send_block(1, t)
+
+    drain(rbuf.at[0], bulk_recv.at[0])
+    attend_block(0, turns[0])
+    for a, b in zip(turns[1:], turns[:-1]):
+        attend_block(0, a)
+        return_block(0, b)
+    return_block(0, turns[-1])
     drain(plane_in, g_recv.at[3])
     drain(plane_in, g_send.at[3])
 
@@ -265,26 +270,20 @@
         ).start()
         return c
 
-    drain(rbuf.at[0], bulk_recv.at[0])
-    attend_block(0, turns[0])
-    lax.fori_loop(1, heads, send_sq, 0)
-    for a, b in zip(turns[1:], turns[:-1]):
-        attend_block(0, a)
-        return_block(0, b)
     drain(rbuf.at[1], bulk_recv.at[1])
     attend_block(1, turns[0])
-    return_block(0, turns[-1])
+    lax.fori_loop(1, heads, send_sq, 0)
     for a, b in zip(turns[1:], turns[:-1]):
         attend_block(1, a)
         return_block(1, b)
 
+    drain(sq_in, sq_send)
+    return_block(1, turns[-1])
     drain(sq_in, sq_recv)
     square = sq_own[...]
     for o in range(1, heads):
         square = square + sq_in[o - 1]
     sq_own_inv = 1.0 / jnp.sqrt(square / (width * heads) + EPSILON)
-    drain(sq_in, sq_send)
-    return_block(1, turns[-1])
     sq_own[...] = sq_own_inv
 
     def scaled(b, c):
@@ -295,34 +294,31 @@
 
     lax.fori_loop(0, count // 128, scaled, 0)
 
-    def taken(frame, here, step):
-        at = ocol[here]
-        lane = lax.broadcasted_iota(jnp.int32, (step, 128), 1).astype(F32)
-        pick = jnp.concatenate(
-            [
-                jnp.where(at == lane + float(frame * frame_rows + b * 128), 1.0, 0.0).astype(BF16)
-                for b in range(frame_rows // 128)
-            ],
-            axis=1,
-        )
-        return nn(pick, ret[frame].reshape(frame_rows, width))
-
-    drain(ret.at[0], back_recv.at[0])
-
-    def first_half(i, c):
-        here = pl.ds(pl.multiple_of(i * 256, 256), 256)
-        y_buf[here] += taken(0, here, 256)
-        return c
-
-    lax.fori_loop(0, count // 256, first_half, 0)
-    drain(ret.at[1], back_recv.at[1])
-
-    def second_half(i, c):
-        here = pl.ds(pl.multiple_of(i * 256, 256), 256)
-        out_ref[here] = (y_buf[here] + taken(1, here, 256)).astype(BF16)
-        return c
-
-    lax.fori_loop(0, count // 256, second_half, 0)
+    def take(frame, turn, last):
+        owners = pl.ds(((cam // GROUP - turn) % blocks) * GROUP, GROUP)
+        first = (frame * frame_rows + ((cam // GROUP - turn) % blocks) * rows).astype(F32)
+        drain(ret.at[frame, owners], back_recv.at[frame, turn])
+
+        def step(i, c):
+            here = pl.ds(pl.multiple_of(i * 256, 256), 256)
+            at = ocol[here] - first
+            lane = lax.broadcasted_iota(jnp.int32, (256, 128), 1).astype(F32)
+            pick = jnp.concatenate(
+                [jnp.where(at == lane + float(b), 1.0, 0.0).astype(BF16) for b in range(0, rows, 128)],
+                axis=1,
+            )
+            got = y_buf[here] + nn(pick, ret[frame, owners].reshape(rows, width))
+            if last:
+                out_ref[here] = got.astype(BF16)
+            else:
+                y_buf[here] = got
+            return c
+
+        lax.fori_loop(0, count // 256, step, 0)
+
+    for frame in range(2):
+        for t in turns:
+            take(frame, t, frame == 1 and t == turns[-1])
     for frame in range(2):
         drain(sbuf.at[frame, pl.ds(0, cams - 1)], bulk_send.at[frame])
         drain(obuf.at[frame, pl.ds(0, cams - 1)], back_send.at[frame])
@@ -350,7 +346,6 @@
             pltpu.VMEM((3, hid, width), F32),
             pltpu.VMEM((PLANE - 1, 3, plane_rows, width), F32),
             pltpu.VMEM((lines - 1, 3, line_rows, width), F32),
-            pltpu.VMEM((3, line_rows, width), F32),
             pltpu.VMEM((3, hid, width), BF16),
             pltpu.VMEM((count, width), F32),
             pltpu.VMEM((count, 128), F32),
@@ -360,7 +355,7 @@
             dma((2,)),
             dma((2,)),
             dma((2,)),
-            dma((2,)),
+            dma((2, cams // GROUP)),
             dma((4,)),
             dma((4,)),
             dma,

time: 145 us -> 137 us (0.945)
  the two profiles are of different devices: /device:TPU:1 before, /device:TPU:5 now
where the time goes in v2:
time: 137 us
  Pallas kernels  135 us (99%)
  local copies, waits for them, and re-layouts  2.26 us (2%)
    pallas_call x1, Pallas kernels, per_device(): pl.pallas_call(functools.partial(layer, cams, heads), out_shape=jax.Shape...  135 us

profile of v2, /device:TPU:5, one launch (start us, length us, event | category | flops | bytes accessed | tf_op | source)
XLA Modules:
  0.0 137.0 jit_solution(9044970268064754346)
XLA Ops:
  0.0 134.8 %layer.1 = bf16[2048,256]{1,0:T(8,128)(2,1)} custom-call(bf16[2048,256]{1,0:T(8,128)(2,1)} %q_ref.1, bf16[2048,256]{1,0:T(8,128)(2,1)} %k_ref.1, bf16[2048,256]{1,0:T(8,128)(2,1)} %v_ref.1, f32[1,2048]{1,0:T(1,128)} %bitcast.8, bf16[256,256]{1,0:T(8,128)(2,1)} %bitcast.5, bf16[256,256]{1,0:T(8,128)(2,1)} %bitcast.6, bf16[256,256]{1,0:T(8,128)(2,1)} %bitcast.7, ...), custom_call_target="tpu_custom_call" | custom-call | tf_op jit(solution)/shard_map/layer/pallas_call | solution.py:335
  134.8 2.3 %copy.11 = bf16[2048,256]{1,0:T(8,128)(2,1)} copy(bf16[2048,256]{1,0:T(8,128)(2,1)} %layer.1) | data formatting | bytes 2097152

commit v3 on v2

--- a/solution.py
+++ b/solution.py
@@ -43,12 +43,13 @@
 
 def layer(
     cams, heads,
-    q_ref, k_ref, v_ref, rates_ref, w1_ref, w3_ref, w2_ref, gain_ref, order_ref,
-    out_ref,
-    sbuf, rbuf, obuf, ret, gbuf, gall, plane_in, line_in, u_buf, y_buf,
+    q_hbm, k_hbm, v_hbm, rates_hbm, w1_hbm, w3_hbm, w2_hbm, gain_hbm, order_hbm,
+    out_hbm,
+    q_ref, k_ref, v_ref, rates_ref, w1_ref, w3_ref, w2_ref, gain_ref, order_ref, out_ref,
+    acc, pick_b, sbuf, rbuf, obuf, ret, gbuf, gall, plane_in, line_in, u_buf, y_buf,
     rcol, ocol, sq_own, sq_in,
     bulk_send, bulk_recv, back_send, back_recv,
-    g_send, g_recv, sq_send, sq_recv,
+    g_send, g_recv, sq_send, sq_recv, in_sem, out_sem,
 ):
     count, width = q_ref.shape
     lines = cams // PLANE
@@ -79,6 +80,27 @@
     lax.fori_loop(1, cams, greet_cam, 0)
     lax.fori_loop(1, heads, greet_head, 0)
 
+    def load(n, src, dst):
+        copy = pltpu.make_async_copy(src, dst, in_sem.at[n])
+        copy.start()
+        return copy
+
+    early = [
+        load(n, src, dst)
+        for n, (src, dst) in enumerate(
+            ((order_hbm, order_ref), (q_hbm, q_ref), (k_hbm, k_ref), (v_hbm, v_ref))
+        )
+    ]
+    later = [
+        load(n + 4, src, dst)
+        for n, (src, dst) in enumerate(
+            (
+                (rates_hbm, rates_ref), (w1_hbm, w1_ref), (w3_hbm, w3_ref),
+                (w2_hbm, w2_ref), (gain_hbm, gain_ref),
+            )
+        )
+    ]
+
     def block_at(turn):
         return (cam // GROUP + turn) % blocks
 
@@ -91,8 +113,10 @@
             got = nn(pick, ref[...]).astype(BF16).reshape(GROUP, PATCHES, width)
             sbuf[frame, pl.ds(blk * GROUP, GROUP), a] = got
 
-    def send_block(frame, turn):
+    def send_block(frame, turn, half=None):
         blk = block_at(turn)
+        low = 1 if turn == 0 else 0
+        low, high = {None: (low, GROUP), 0: (low, GROUP // 2), 1: (GROUP // 2, GROUP)}[half]
 
         def one(j, c):
             dest = blk * GROUP + (cam + j) % GROUP
@@ -106,11 +130,11 @@
             ).start()
             return c
 
-        if turn == 0:
+        if turn == 0 and half != 1:
             pltpu.make_async_copy(
                 sbuf.at[frame, cam], rbuf.at[frame, cam], bulk_recv.at[frame]
             ).start()
-        lax.fori_loop(1 if turn == 0 else 0, GROUP, one, 0)
+        lax.fori_loop(low, high, one, 0)
 
     def attend_block(frame, turn):
         blk = block_at(turn)
@@ -132,7 +156,7 @@
                 src_ref=obuf.at[frame, dest],
                 dst_ref=ret.at[frame, cam],
                 send_sem=back_send.at[frame],
-                recv_sem=back_recv.at[frame, turn],
+                recv_sem=back_recv.at[frame],
                 device_id=(dest, head),
                 device_id_type=MESH,
             ).start()
@@ -140,7 +164,7 @@
 
         if turn == 0:
             pltpu.make_async_copy(
-                obuf.at[frame, cam], ret.at[frame, cam], back_recv.at[frame, turn]
+                obuf.at[frame, cam], ret.at[frame, cam], back_recv.at[frame]
             ).start()
         lax.fori_loop(1 if turn == 0 else 0, GROUP, one, 0)
 
@@ -170,6 +194,22 @@
         gbuf[2] += nn(act, err)
         return c
 
+    def pick_of(frame, here, step):
+        at = ocol[here]
+        lane = lax.broadcasted_iota(jnp.int32, (step, 128), 1).astype(F32)
+        return jnp.concatenate(
+            [
+                jnp.where(at == lane + float(frame * frame_rows + b), 1.0, 0.0).astype(BF16)
+                for b in range(0, frame_rows, 128)
+            ],
+            axis=1,
+        )
+
+    def build_pick(i, c):
+        here = pl.ds(pl.multiple_of(i * 256, 256), 256)
+        pick_b[here] = pick_of(1, here, 256)
+        return c
+
     def plane_peer(o):
         return (line * PLANE + (place + o) % PLANE, head)
 
@@ -182,35 +222,53 @@
             device_id=peer, device_id_type=MESH,
         ).start()
 
+    far, sides, near = turns[:1], turns[1:-1], turns[-1:]
+    if len(turns) == 1:
+        far, near = turns, []
+
+    for copy in early:
+        copy.wait()
+    for t in far:
+        sort_block(0, t)
+    pl.semaphore_wait(barrier, cams - 1 + heads - 1)
+    for t in far:
+        send_block(0, t)
+
+    for copy in later:
+        copy.wait()
     lax.fori_loop(0, count // 128, columns, 0)
     u_buf[0] = jnp.transpose(w2_ref[...].astype(F32)).astype(BF16)
     gbuf[...] = jnp.zeros_like(gbuf)
     lax.fori_loop(0, count // 512, grad_step, 0)
-    sort_block(0, turns[0])
-    pl.semaphore_wait(barrier, cams - 1 + heads - 1)
-
+    for t in sides[:1]:
+        sort_block(0, t)
     for o in range(1, PLANE):
         theirs = pl.ds(((place + o) % PLANE) * plane_rows, plane_rows)
         stage(0, gbuf.at[:, theirs], plane_in.at[o - 1], plane_peer(o))
-    send_block(0, turns[0])
-    for t in turns[1:2]:
+    for t in sides[1:]:
         sort_block(0, t)
-        send_block(0, t)
+    for t in sides:
+        send_block(0, t, 0)
+    for t in near:
+        sort_block(0, t)
+    for t in far:
+        sort_block(1, t)
     drain(plane_in, g_recv.at[0])
     drain(plane_in, g_send.at[0])
     mine = pl.ds(place * plane_rows, plane_rows)
     gbuf[:, mine] += plane_in[0] + plane_in[1] + plane_in[2]
 
-    for t in turns[2:3]:
-        sort_block(0, t)
+    for t in sides[:1]:
+        sort_block(1, t)
     for o in range(1, lines):
         theirs = pl.ds(place * plane_rows + ((line + o) % lines) * line_rows, line_rows)
         stage(1, gbuf.at[:, theirs], line_in.at[o - 1], line_peer(o))
-    for t in turns[2:3]:
+    for t in sides:
+        send_block(0, t, 1)
+    for t in near:
         send_block(0, t)
-    for t in turns[3:]:
-        sort_block(0, t)
-        send_block(0, t)
+    for t in sides[1:] + near:
+        sort_block(1, t)
     drain(line_in, g_recv.at[1])
     drain(line_in, g_send.at[1])
     own = pl.ds(place * plane_rows + line * line_rows, line_rows)
@@ -218,20 +276,17 @@
     for o in range(1, lines):
         total = total + line_in[o - 1]
     gall[:, own] = total
-    sort_block(1, turns[0])
+    lax.fori_loop(0, count // 256, build_pick, 0)
 
     for o in range(1, lines):
         stage(2, gall.at[:, own], gall.at[:, own], line_peer(o))
-    send_block(1, turns[0])
-    for t in turns[1:2]:
-        sort_block(1, t)
+    for t in far:
         send_block(1, t)
     drain(line_in, g_recv.at[2])
     drain(line_in, g_send.at[2])
     for o in range(1, PLANE):
         stage(3, gall.at[:, mine], gall.at[:, mine], plane_peer(o))
-    for t in turns[2:]:
-        sort_block(1, t)
+    for t in sides + near:
         send_block(1, t)
 
     drain(rbuf.at[0], bulk_recv.at[0])
@@ -276,49 +331,42 @@
     for a, b in zip(turns[1:], turns[:-1]):
         attend_block(1, a)
         return_block(1, b)
+    return_block(1, turns[-1])
+
+    drain(ret.at[0], back_recv.at[0])
+
+    def first_half(i, c):
+        here = pl.ds(pl.multiple_of(i * 256, 256), 256)
+        acc[here] = nn(pick_of(0, here, 256), ret[0].reshape(frame_rows, width))
+        return c
+
+    lax.fori_loop(0, count // 256, first_half, 0)
 
     drain(sq_in, sq_send)
-    return_block(1, turns[-1])
     drain(sq_in, sq_recv)
     square = sq_own[...]
     for o in range(1, heads):
         square = square + sq_in[o - 1]
-    sq_own_inv = 1.0 / jnp.sqrt(square / (width * heads) + EPSILON)
-    sq_own[...] = sq_own_inv
+    sq_own[...] = 1.0 / jnp.sqrt(square / (width * heads) + EPSILON)
 
     def scaled(b, c):
         here = pl.ds(pl.multiple_of(b * 128, 128), 128)
         inv = column_of(sq_own[pl.ds(b, 1)])
-        y_buf[here] = y_buf[here] * jnp.concatenate([inv, inv], axis=1) * gain_ref[...]
+        acc[here] += y_buf[here] * jnp.concatenate([inv, inv], axis=1) * gain_ref[...]
         return c
 
     lax.fori_loop(0, count // 128, scaled, 0)
-
-    def take(frame, turn, last):
-        owners = pl.ds(((cam // GROUP - turn) % blocks) * GROUP, GROUP)
-        first = (frame * frame_rows + ((cam // GROUP - turn) % blocks) * rows).astype(F32)
-        drain(ret.at[frame, owners], back_recv.at[frame, turn])
-
-        def step(i, c):
-            here = pl.ds(pl.multiple_of(i * 256, 256), 256)
-            at = ocol[here] - first
-            lane = lax.broadcasted_iota(jnp.int32, (256, 128), 1).astype(F32)
-            pick = jnp.concatenate(
-                [jnp.where(at == lane + float(b), 1.0, 0.0).astype(BF16) for b in range(0, rows, 128)],
-                axis=1,
-            )
-            got = y_buf[here] + nn(pick, ret[frame, owners].reshape(rows, width))
-            if last:
-                out_ref[here] = got.astype(BF16)
-            else:
-                y_buf[here] = got
-            return c
-
-        lax.fori_loop(0, count // 256, step, 0)
-
-    for frame in range(2):
-        for t in turns:
-            take(frame, t, frame == 1 and t == turns[-1])
+    drain(ret.at[1], back_recv.at[1])
+
+    def second_half(i, c):
+        here = pl.ds(pl.multiple_of(i * 256, 256), 256)
+        taken = nn(pick_b[here], ret[1].reshape(frame_rows, width))
+        out_ref[here] = (acc[here] + taken).astype(BF16)
+        pltpu.make_async_copy(out_ref.at[here], out_hbm.at[here], out_sem).start()
+        return c
+
+    lax.fori_loop(0, count // 256, second_half, 0)
+    drain(out_ref, out_sem)
     for frame in range(2):
         drain(sbuf.at[frame, pl.ds(0, cams - 1)], bulk_send.at[frame])
         drain(obuf.at[frame, pl.ds(0, cams - 1)], back_send.at[frame])
@@ -331,13 +379,25 @@
     lines = cams // PLANE
     line_rows = plane_rows // lines
     dma = pltpu.SemaphoreType.DMA
-    vmem = pl.BlockSpec(memory_space=pltpu.VMEM)
+    hbm = pl.BlockSpec(memory_space=pl.ANY)
     return pl.pallas_call(
         functools.partial(layer, cams, heads),
         out_shape=jax.ShapeDtypeStruct((count, width), BF16),
-        in_specs=[vmem] * 9,
-        out_specs=vmem,
+        in_specs=[hbm] * 9,
+        out_specs=hbm,
         scratch_shapes=[
+            pltpu.VMEM((count, width), BF16),
+            pltpu.VMEM((count, width), BF16),
+            pltpu.VMEM((count, width), BF16),
+            pltpu.VMEM((1, count), F32),
+            pltpu.VMEM((hid, width), BF16),
+            pltpu.VMEM((hid, width), BF16),
+            pltpu.VMEM((width, hid), BF16),
+            pltpu.VMEM((1, width), F32),
+            pltpu.VMEM((1, count), jnp.int32),
+            pltpu.VMEM((count, width), BF16),
+            pltpu.VMEM((count, width), F32),
+            pltpu.VMEM((count, cams * PATCHES), BF16),
             pltpu.VMEM((2, cams, 3, PATCHES, width), BF16),
             pltpu.VMEM((2, cams, 3, PATCHES, width), BF16),
             pltpu.VMEM((2, cams, PATCHES, width), BF16),
@@ -355,10 +415,12 @@
             dma((2,)),
             dma((2,)),
             dma((2,)),
-            dma((2, cams // GROUP)),
+            dma((2,)),
             dma((4,)),
             dma((4,)),
             dma,
+            dma,
+            dma((9,)),
             dma,
         ],
         compiler_params=pltpu.CompilerParams(

time: 137 us -> 124 us (0.905)
  the two profiles are of different devices: /device:TPU:5 before, /device:TPU:1 now
where the time goes in v3:
time: 124 us
  Pallas kernels  122 us (98%)
  local copies, waits for them, and re-layouts  2.26 us (2%)
    pallas_call x1, Pallas kernels, per_device(): pl.pallas_call(functools.partial(layer, cams, heads), out_shape=jax.Shape...  122 us

profile of v3, /device:TPU:1, one launch (start us, length us, event | category | flops | bytes accessed | tf_op | source)
XLA Modules:
  0.0 124.2 jit_solution(7194435738964240385)
XLA Ops:
  0.0 121.9 %layer.1 = bf16[2048,256]{1,0:T(8,128)(2,1)} custom-call(bf16[2048,256]{1,0:T(8,128)(2,1)} %q_hbm.1, bf16[2048,256]{1,0:T(8,128)(2,1)} %k_hbm.1, bf16[2048,256]{1,0:T(8,128)(2,1)} %v_hbm.1, f32[1,2048]{1,0:T(1,128)} %bitcast.8, bf16[256,256]{1,0:T(8,128)(2,1)} %bitcast.5, bf16[256,256]{1,0:T(8,128)(2,1)} %bitcast.6, bf16[256,256]{1,0:T(8,128)(2,1)} %bitcast.7, ...), custom_call_target="tpu_custom_call" | custom-call | tf_op jit(solution)/shard_map/layer/pallas_call | solution.py:383
  121.9 2.3 %copy.11 = bf16[2048,256]{1,0:T(8,128)(2,1)} copy(bf16[2048,256]{1,0:T(8,128)(2,1)} %layer.1) | data formatting | bytes 2097152

commit v4 on v3

--- a/solution.py
+++ b/solution.py
@@ -31,25 +31,29 @@
     pltpu.make_async_copy(ref, ref, sem).wait()
 
 
-def renewed(weight, grad):
+def mean_square(weight):
     wf = weight.astype(F32)
-    scale = jnp.sqrt(jnp.mean(wf * wf)) / jnp.sqrt(jnp.mean(grad * grad) + EPSILON)
-    moved = wf - scale * grad
-    ratio = jnp.sqrt(jnp.sum(wf * wf, axis=1, keepdims=True)) / jnp.sqrt(
+    return jnp.mean(wf * wf)
+
+
+def renewed(rows, grad, weight_square, grad_square):
+    scale = jnp.sqrt(weight_square) / jnp.sqrt(grad_square + EPSILON)
+    moved = rows - scale * grad
+    ratio = jnp.sqrt(jnp.sum(rows * rows, axis=1, keepdims=True)) / jnp.sqrt(
         jnp.sum(moved * moved, axis=1, keepdims=True) + EPSILON
     )
-    return (moved * ratio).astype(BF16)
+    return moved * ratio
 
 
 def layer(
     cams, heads,
     q_hbm, k_hbm, v_hbm, rates_hbm, w1_hbm, w3_hbm, w2_hbm, gain_hbm, order_hbm,
-    out_hbm,
-    q_ref, k_ref, v_ref, rates_ref, w1_ref, w3_ref, w2_ref, gain_ref, order_ref, out_ref,
-    acc, pick_b, sbuf, rbuf, obuf, ret, gbuf, gall, plane_in, line_in, u_buf, y_buf,
+    out_ref,
+    q_ref, k_ref, v_ref, rates_ref, w1_ref, w3_ref, w2_ref, gain_ref, order_ref,
+    acc, pick_b, w32, line_own, sums_own, sums_in, sbuf, rbuf, obuf, ret, gbuf, gall, plane_in, line_in, u_buf, y_buf,
     rcol, ocol, sq_own, sq_in,
     bulk_send, bulk_recv, back_send, back_recv,
-    g_send, g_recv, sq_send, sq_recv, in_sem, out_sem,
+    g_send, g_recv, sq_send, sq_recv, in_sem, sums_send, sums_recv,
 ):
     count, width = q_ref.shape
     lines = cams // PLANE
@@ -63,23 +67,6 @@
     head = lax.axis_index("head")
     line, place = cam // PLANE, cam % PLANE
 
-    barrier = pltpu.get_barrier_semaphore()
-
-    def greet_cam(o, c):
-        pl.semaphore_signal(
-            barrier, inc=1, device_id=((cam + o) % cams, head), device_id_type=MESH
-        )
-        return c
-
-    def greet_head(o, c):
-        pl.semaphore_signal(
-            barrier, inc=1, device_id=(cam, (head + o) % heads), device_id_type=MESH
-        )
-        return c
-
-    lax.fori_loop(1, cams, greet_cam, 0)
-    lax.fori_loop(1, heads, greet_head, 0)
-
     def load(n, src, dst):
         copy = pltpu.make_async_copy(src, dst, in_sem.at[n])
         copy.start()
@@ -91,6 +78,23 @@
             ((order_hbm, order_ref), (q_hbm, q_ref), (k_hbm, k_ref), (v_hbm, v_ref))
         )
     ]
+    barrier = pltpu.get_barrier_semaphore()
+
+    def greet_cam(o, c):
+        pl.semaphore_signal(
+            barrier, inc=1, device_id=((cam + o) % cams, head), device_id_type=MESH
+        )
+        return c
+
+    def greet_head(o, c):
+        pl.semaphore_signal(
+            barrier, inc=1, device_id=(cam, (head + o) % heads), device_id_type=MESH
+        )
+        return c
+
+    lax.fori_loop(1, cams, greet_cam, 0)
+    lax.fori_loop(1, heads, greet_head, 0)
+
     later = [
         load(n + 4, src, dst)
         for n, (src, dst) in enumerate(
@@ -156,7 +160,7 @@
                 src_ref=obuf.at[frame, dest],
                 dst_ref=ret.at[frame, cam],
                 send_sem=back_send.at[frame],
-                recv_sem=back_recv.at[frame],
+                recv_sem=back_recv.at[frame, turn],
                 device_id=(dest, head),
                 device_id_type=MESH,
             ).start()
@@ -164,7 +168,7 @@
 
         if turn == 0:
             pltpu.make_async_copy(
-                obuf.at[frame, cam], ret.at[frame, cam], back_recv.at[frame]
+                obuf.at[frame, cam], ret.at[frame, cam], back_recv.at[frame, turn]
             ).start()
         lax.fori_loop(1 if turn == 0 else 0, GROUP, one, 0)
 
@@ -207,7 +211,9 @@
 
     def build_pick(i, c):
         here = pl.ds(pl.multiple_of(i * 256, 256), 256)
-        pick_b[here] = pick_of(1, here, 256)
+        pick = pick_of(1, here, 256)
+        for b in range(blocks):
+            pick_b[b, here] = pick[:, b * rows : (b + 1) * rows]
         return c
 
     def plane_peer(o):
@@ -237,9 +243,12 @@
     for copy in later:
         copy.wait()
     lax.fori_loop(0, count // 128, columns, 0)
-    u_buf[0] = jnp.transpose(w2_ref[...].astype(F32)).astype(BF16)
+    for m, w in enumerate((w1_ref, w3_ref, w2_ref)):
+        w32[m] = w[...].astype(F32)
+    u_buf[0] = jnp.transpose(w32[2]).astype(BF16)
     gbuf[...] = jnp.zeros_like(gbuf)
     lax.fori_loop(0, count // 512, grad_step, 0)
+    gbuf[2] = jnp.transpose(gbuf[2])
     for t in sides[:1]:
         sort_block(0, t)
     for o in range(1, PLANE):
@@ -267,6 +276,8 @@
         send_block(0, t, 1)
     for t in near:
         send_block(0, t)
+    for t in far:
+        send_block(1, t, 0)
     for t in sides[1:] + near:
         sort_block(1, t)
     drain(line_in, g_recv.at[1])
@@ -275,18 +286,47 @@
     total = gbuf[:, own]
     for o in range(1, lines):
         total = total + line_in[o - 1]
-    gall[:, own] = total
+    lane = lax.broadcasted_iota(jnp.int32, (1, 128), 1)
+    squares = jnp.zeros((1, 128), F32)
+    for m in range(3):
+        squares = jnp.where(lane == m, jnp.sum(total[m] * total[m]), squares)
+    sums_own[...] = squares
+    line_own[...] = total
+
+    def send_sums(o, c):
+        pltpu.make_async_remote_copy(
+            src_ref=sums_own, dst_ref=sums_in.at[o - 1],
+            send_sem=sums_send, recv_sem=sums_recv,
+            device_id=((cam + o) % cams, head), device_id_type=MESH,
+        ).start()
+        return c
+
     lax.fori_loop(0, count // 256, build_pick, 0)
+    lax.fori_loop(1, cams, send_sums, 0)
+    for t in far:
+        send_block(1, t, 1)
+    for t in sides:
+        send_block(1, t, 0)
+    weight_squares = [mean_square(w[...]) for w in (w1_ref, w3_ref, w2_ref)]
+    drain(sums_in, sums_recv)
+    drain(sums_in, sums_send)
+    squares = sums_own[...] + jnp.sum(sums_in[...], axis=0)
+    for m, w in enumerate((w1_ref, w3_ref, w2_ref)):
+        square = jnp.sum(jnp.where(lane == m, squares, 0.0)) / (hid * width)
+        piece = renewed(w32[m, own], line_own[m], weight_squares[m], square)
+        gall[place, line, m] = jnp.concatenate(
+            [piece[:, :128], piece[:, 128:]], axis=0
+        ).astype(BF16)
 
     for o in range(1, lines):
-        stage(2, gall.at[:, own], gall.at[:, own], line_peer(o))
-    for t in far:
-        send_block(1, t)
-    drain(line_in, g_recv.at[2])
-    drain(line_in, g_send.at[2])
+        stage(2, gall.at[place, line], gall.at[place, line], line_peer(o))
+    for t in sides:
+        send_block(1, t, 1)
+    drain(gall.at[0, pl.ds(0, lines - 1)], g_recv.at[2])
+    drain(gall.at[0, pl.ds(0, lines - 1)], g_send.at[2])
     for o in range(1, PLANE):
-        stage(3, gall.at[:, mine], gall.at[:, mine], plane_peer(o))
-    for t in sides + near:
+        stage(3, gall.at[place], gall.at[place], plane_peer(o))
+    for t in near:
         send_block(1, t)
 
     drain(rbuf.at[0], bulk_recv.at[0])
@@ -295,12 +335,23 @@
         attend_block(0, a)
         return_block(0, b)
     return_block(0, turns[-1])
-    drain(plane_in, g_recv.at[3])
-    drain(plane_in, g_send.at[3])
-
-    u_buf[0] = renewed(w1_ref[...], gall[0])
-    u_buf[1] = renewed(w3_ref[...], gall[1])
-    u_buf[2] = renewed(w2_ref[...], jnp.transpose(gall[2]))
+
+    drain(rbuf.at[1], bulk_recv.at[1])
+    attend_block(1, turns[0])
+    for a, b in zip(turns[1:], turns[:-1]):
+        attend_block(1, a)
+        return_block(1, b)
+    return_block(1, turns[-1])
+
+    drain(gall.at[pl.ds(0, PLANE - 1)], g_recv.at[3])
+    drain(gall.at[pl.ds(0, PLANE - 1)], g_send.at[3])
+    for m in range(3):
+        for p in range(PLANE):
+            for n in range(lines):
+                at = pl.ds(p * plane_rows + n * line_rows, line_rows)
+                piece = gall[p, n, m].astype(F32)
+                gbuf[m, at] = jnp.concatenate([piece[:line_rows], piece[line_rows:]], axis=1)
+    u_buf[...] = gbuf[...].astype(BF16)
 
     def readout(i, c):
         step = 256
@@ -309,7 +360,7 @@
         q1, q3 = nt(query, u_buf[0]), nt(query, u_buf[1])
         act = (q1 * jax.nn.sigmoid(q1) * q3).astype(BF16)
         y = nt(act, u_buf[2])
-        y_buf[here] = y
+        y_buf[here] = y * gain_ref[...]
         half = y[:, :128] * y[:, :128] + y[:, 128:] * y[:, 128:]
         for b in range(step // 128):
             part = jnp.sum(jnp.transpose(half[b * 128 : (b + 1) * 128]), axis=0, keepdims=True)
@@ -325,15 +376,16 @@
         ).start()
         return c
 
-    drain(rbuf.at[1], bulk_recv.at[1])
-    attend_block(1, turns[0])
     lax.fori_loop(1, heads, send_sq, 0)
-    for a, b in zip(turns[1:], turns[:-1]):
-        attend_block(1, a)
-        return_block(1, b)
-    return_block(1, turns[-1])
-
-    drain(ret.at[0], back_recv.at[0])
+
+    def owners_at(turn):
+        return (cam // GROUP - turn) % blocks
+
+    def await_return(frame, turn):
+        drain(ret.at[frame, pl.ds(owners_at(turn) * GROUP, GROUP)], back_recv.at[frame, turn])
+
+    for t in turns:
+        await_return(0, t)
 
     def first_half(i, c):
         here = pl.ds(pl.multiple_of(i * 256, 256), 256)
@@ -351,22 +403,24 @@
 
     def scaled(b, c):
         here = pl.ds(pl.multiple_of(b * 128, 128), 128)
-        inv = column_of(sq_own[pl.ds(b, 1)])
-        acc[here] += y_buf[here] * jnp.concatenate([inv, inv], axis=1) * gain_ref[...]
+        rcol[here] = column_of(sq_own[pl.ds(b, 1)])
         return c
 
     lax.fori_loop(0, count // 128, scaled, 0)
-    drain(ret.at[1], back_recv.at[1])
+
+    for t in turns:
+        await_return(1, t)
 
     def second_half(i, c):
-        here = pl.ds(pl.multiple_of(i * 256, 256), 256)
-        taken = nn(pick_b[here], ret[1].reshape(frame_rows, width))
-        out_ref[here] = (acc[here] + taken).astype(BF16)
-        pltpu.make_async_copy(out_ref.at[here], out_hbm.at[here], out_sem).start()
-        return c
-
-    lax.fori_loop(0, count // 256, second_half, 0)
-    drain(out_ref, out_sem)
+        here = pl.ds(pl.multiple_of(i * 512, 512), 512)
+        inv = rcol[here]
+        got = acc[here] + y_buf[here] * jnp.concatenate([inv, inv], axis=1)
+        for b in range(blocks):
+            got += nn(pick_b[b, here], ret[1, b * GROUP : (b + 1) * GROUP].reshape(rows, width))
+        out_ref[here] = got.astype(BF16)
+        return c
+
+    lax.fori_loop(0, count // 512, second_half, 0)
     for frame in range(2):
         drain(sbuf.at[frame, pl.ds(0, cams - 1)], bulk_send.at[frame])
         drain(obuf.at[frame, pl.ds(0, cams - 1)], back_send.at[frame])
@@ -382,9 +436,9 @@
     hbm = pl.BlockSpec(memory_space=pl.ANY)
     return pl.pallas_call(
         functools.partial(layer, cams, heads),
-        out_shape=jax.ShapeDtypeStruct((count, width), BF16),
+        out_shape=pltpu.VMEM((count, width), BF16),
         in_specs=[hbm] * 9,
-        out_specs=hbm,
+        out_specs=pl.BlockSpec(memory_space=pltpu.VMEM),
         scratch_shapes=[
             pltpu.VMEM((count, width), BF16),
             pltpu.VMEM((count, width), BF16),
@@ -395,15 +449,18 @@
             pltpu.VMEM((width, hid), BF16),
             pltpu.VMEM((1, width), F32),
             pltpu.VMEM((1, count), jnp.int32),
-            pltpu.VMEM((count, width), BF16),
             pltpu.VMEM((count, width), F32),
-            pltpu.VMEM((count, cams * PATCHES), BF16),
+            pltpu.VMEM((cams // GROUP, count, GROUP * PATCHES), BF16),
+            pltpu.VMEM((3, hid, width), F32),
+            pltpu.VMEM((3, line_rows, width), F32),
+            pltpu.VMEM((1, 128), F32),
+            pltpu.VMEM((cams - 1, 1, 128), F32),
             pltpu.VMEM((2, cams, 3, PATCHES, width), BF16),
             pltpu.VMEM((2, cams, 3, PATCHES, width), BF16),
             pltpu.VMEM((2, cams, PATCHES, width), BF16),
             pltpu.VMEM((2, cams, PATCHES, width), BF16),
             pltpu.VMEM((3, hid, width), F32),
-            pltpu.VMEM((3, hid, width), F32),
+            pltpu.VMEM((PLANE, lines, 3, 2 * line_rows, width // 2), BF16),
             pltpu.VMEM((PLANE - 1, 3, plane_rows, width), F32),
             pltpu.VMEM((lines - 1, 3, line_rows, width), F32),
             pltpu.VMEM((3, hid, width), BF16),
@@ -415,12 +472,13 @@
             dma((2,)),
             dma((2,)),
             dma((2,)),
-            dma((2,)),
+            dma((2, cams // GROUP)),
             dma((4,)),
             dma((4,)),
             dma,
             dma,
             dma((9,)),
+            dma,
             dma,
         ],
         compiler_params=pltpu.CompilerParams(

time: 124 us -> 122 us (0.984)
  local copies, waits for them, and re-layouts: 2.26 us -> 0.97 us
    unnamed x1, local copies, waits for them, and re-layouts: 2.26 us -> 0.97 us
where the time goes in v4:
time: 122 us
  Pallas kernels  121 us (99%)
    pallas_call x1, Pallas kernels, per_device(): pl.pallas_call(functools.partial(layer, cams, heads), out_shape=pltpu.VME...  121 us

profile of v4, /device:TPU:1, one launch (start us, length us, event | category | flops | bytes accessed | tf_op | source)
XLA Modules:
  0.0 122.0 jit_solution(16234269380289007708)
XLA Ops:
  0.0 121.0 %layer.1 = bf16[2048,256]{1,0:T(8,128)(2,1)S(1)} custom-call(bf16[2048,256]{1,0:T(8,128)(2,1)} %q_hbm.1, bf16[2048,256]{1,0:T(8,128)(2,1)} %k_hbm.1, bf16[2048,256]{1,0:T(8,128)(2,1)} %v_hbm.1, f32[1,2048]{1,0:T(1,128)} %bitcast.8, bf16[256,256]{1,0:T(8,128)(2,1)} %bitcast.5, bf16[256,256]{1,0:T(8,128)(2,1)} %bitcast.6, bf16[256,256]{1,0:T(8,128)(2,1)} %bitcast.7, ...), custom_call_target="tpu_custom_call" | custom-call | tf_op jit(solution)/shard_map/layer/pallas_call | solution.py:437
  121.0 1.0 copy.11

commit v5 on v4

--- a/solution.py
+++ b/solution.py
@@ -81,9 +81,8 @@
     barrier = pltpu.get_barrier_semaphore()
 
     def greet_cam(o, c):
-        pl.semaphore_signal(
-            barrier, inc=1, device_id=((cam + o) % cams, head), device_id_type=MESH
-        )
+        peer = (cam + cams // 2 + o) % cams
+        pl.semaphore_signal(barrier, inc=1, device_id=(peer, head), device_id_type=MESH)
         return c
 
     def greet_head(o, c):
@@ -92,7 +91,8 @@
         )
         return c
 
-    lax.fori_loop(1, cams, greet_cam, 0)
+    lax.fori_loop(0, cams // 2, greet_cam, 0)
+    lax.fori_loop(cams // 2 + 1, cams, greet_cam, 0)
     lax.fori_loop(1, heads, greet_head, 0)
 
     later = [
@@ -108,12 +108,14 @@
     def block_at(turn):
         return (cam // GROUP + turn) % blocks
 
-    def sort_block(frame, turn):
+    def sort_block(frame, turn, arriving=(None, None, None)):
         blk = block_at(turn)
         first = frame * frame_rows + blk * rows
         slot = lax.broadcasted_iota(jnp.int32, (rows, count), 0) + first
         pick = jnp.where(slot == order_ref[...], 1.0, 0.0).astype(BF16)
         for a, ref in enumerate((q_ref, k_ref, v_ref)):
+            if arriving[a] is not None:
+                arriving[a].wait()
             got = nn(pick, ref[...]).astype(BF16).reshape(GROUP, PATCHES, width)
             sbuf[frame, pl.ds(blk * GROUP, GROUP), a] = got
 
@@ -232,10 +234,9 @@
     if len(turns) == 1:
         far, near = turns, []
 
-    for copy in early:
-        copy.wait()
+    early[0].wait()
     for t in far:
-        sort_block(0, t)
+        sort_block(0, t, early[1:])
     pl.semaphore_wait(barrier, cams - 1 + heads - 1)
     for t in far:
         send_block(0, t)
@@ -301,12 +302,14 @@
         ).start()
         return c
 
-    lax.fori_loop(0, count // 256, build_pick, 0)
     lax.fori_loop(1, cams, send_sums, 0)
     for t in far:
         send_block(1, t, 1)
     for t in sides:
         send_block(1, t, 0)
+    drain(rbuf.at[0], bulk_recv.at[0])
+    for t in turns:
+        attend_block(0, t)
     weight_squares = [mean_square(w[...]) for w in (w1_ref, w3_ref, w2_ref)]
     drain(sums_in, sums_recv)
     drain(sums_in, sums_send)
@@ -322,19 +325,15 @@
         stage(2, gall.at[place, line], gall.at[place, line], line_peer(o))
     for t in sides:
         send_block(1, t, 1)
+    for t in near:
+        send_block(1, t)
+    for t in turns:
+        return_block(0, t)
     drain(gall.at[0, pl.ds(0, lines - 1)], g_recv.at[2])
     drain(gall.at[0, pl.ds(0, lines - 1)], g_send.at[2])
     for o in range(1, PLANE):
         stage(3, gall.at[place], gall.at[place], plane_peer(o))
-    for t in near:
-        send_block(1, t)
-
-    drain(rbuf.at[0], bulk_recv.at[0])
-    attend_block(0, turns[0])
-    for a, b in zip(turns[1:], turns[:-1]):
-        attend_block(0, a)
-        return_block(0, b)
-    return_block(0, turns[-1])
+    lax.fori_loop(0, count // 256, build_pick, 0)
 
     drain(rbuf.at[1], bulk_recv.at[1])
     attend_block(1, turns[0])

time: 122 us -> 120 us (0.984)
  Pallas kernels: 121 us -> 119 us
    pallas_call x1, Pallas kernels: 121 us -> 119 us  [per_device(): pl.pallas_call(functools.partial(layer, cams, heads), out_shape=pltpu.VME...]
where the time goes in v5:
time: 120 us
  Pallas kernels  119 us (99%)
    pallas_call x1, Pallas kernels, per_device(): pl.pallas_call(functools.partial(layer, cams, heads), out_shape=pltpu.VME...  119 us

profile of v5, /device:TPU:1, one launch (start us, length us, event | category | flops | bytes accessed | tf_op | source)
XLA Modules:
  0.0 120.1 jit_solution(8410550579384797137)
XLA Ops:
  0.0 119.1 %layer.1 = bf16[2048,256]{1,0:T(8,128)(2,1)S(1)} custom-call(bf16[2048,256]{1,0:T(8,128)(2,1)} %q_hbm.1, bf16[2048,256]{1,0:T(8,128)(2,1)} %k_hbm.1, bf16[2048,256]{1,0:T(8,128)(2,1)} %v_hbm.1, f32[1,2048]{1,0:T(1,128)} %bitcast.8, bf16[256,256]{1,0:T(8,128)(2,1)} %bitcast.5, bf16[256,256]{1,0:T(8,128)(2,1)} %bitcast.6, bf16[256,256]{1,0:T(8,128)(2,1)} %bitcast.7, ...), custom_call_target="tpu_custom_call" | custom-call | tf_op jit(solution)/shard_map/layer/pallas_call | solution.py:436
  119.1 1.0 copy.11

commit v6 on v5

--- a/solution.py
+++ b/solution.py
@@ -261,22 +261,20 @@
         send_block(0, t, 0)
     for t in near:
         sort_block(0, t)
-    for t in far:
+    for t in near:
+        send_block(0, t)
+    for t in far + sides[:1]:
         sort_block(1, t)
     drain(plane_in, g_recv.at[0])
     drain(plane_in, g_send.at[0])
     mine = pl.ds(place * plane_rows, plane_rows)
     gbuf[:, mine] += plane_in[0] + plane_in[1] + plane_in[2]
 
-    for t in sides[:1]:
-        sort_block(1, t)
     for o in range(1, lines):
         theirs = pl.ds(place * plane_rows + ((line + o) % lines) * line_rows, line_rows)
         stage(1, gbuf.at[:, theirs], line_in.at[o - 1], line_peer(o))
     for t in sides:
         send_block(0, t, 1)
-    for t in near:
-        send_block(0, t)
     for t in far:
         send_block(1, t, 0)
     for t in sides[1:] + near:
@@ -410,8 +408,10 @@
     for t in turns:
         await_return(1, t)
 
+    tail = min(count, 1024)
+
     def second_half(i, c):
-        here = pl.ds(pl.multiple_of(i * 512, 512), 512)
+        here = pl.ds(pl.multiple_of(i * tail, tail), tail)
         inv = rcol[here]
         got = acc[here] + y_buf[here] * jnp.concatenate([inv, inv], axis=1)
         for b in range(blocks):
@@ -419,7 +419,7 @@
         out_ref[here] = got.astype(BF16)
         return c
 
-    lax.fori_loop(0, count // 512, second_half, 0)
+    lax.fori_loop(0, count // tail, second_half, 0)
     for frame in range(2):
         drain(sbuf.at[frame, pl.ds(0, cams - 1)], bulk_send.at[frame])
         drain(obuf.at[frame, pl.ds(0, cams - 1)], back_send.at[frame])

time: 120 us -> 120 us (level)
  no operation moved by 1% of the time
where the time goes in v6:
time: 120 us
  Pallas kernels  119 us (99%)
    pallas_call x1, Pallas kernels, per_device(): pl.pallas_call(functools.partial(layer, cams, heads), out_shape=pltpu.VME...  119 us

profile of v6, /device:TPU:1, one launch (start us, length us, event | category | flops | bytes accessed | tf_op | source)
XLA Modules:
  0.0 119.6 jit_solution(2619198898207646086)
XLA Ops:
  0.0 118.7 %layer.1 = bf16[2048,256]{1,0:T(8,128)(2,1)S(1)} custom-call(bf16[2048,256]{1,0:T(8,128)(2,1)} %q_hbm.1, bf16[2048,256]{1,0:T(8,128)(2,1)} %k_hbm.1, bf16[2048,256]{1,0:T(8,128)(2,1)} %v_hbm.1, f32[1,2048]{1,0:T(1,128)} %bitcast.8, bf16[256,256]{1,0:T(8,128)(2,1)} %bitcast.5, bf16[256,256]{1,0:T(8,128)(2,1)} %bitcast.6, bf16[256,256]{1,0:T(8,128)(2,1)} %bitcast.7, ...), custom_call_target="tpu_custom_call" | custom-call | tf_op jit(solution)/shard_map/layer/pallas_call | solution.py:436
  118.7 1.0 copy.11
